TPU v7x, 32 devices: a whole 2x2x4 slice. The times are simulated.
32 devices in a mesh: view: 4 (over y, core), row: 8 (over z, x).
Axes of the slice: x: 2, y: 2, z: 4, core: 2. Of those that a mesh axis runs over, the one named last changes fastest.
Arguments:
- features: float32 [4, 16384, 2048], P('view', 'row'), may hold values from -0.125 to 0.125
- view_maps: float32 [4, 2048, 256], P('view', 'row'), may hold values from -6 to 6
- shared: float32 [16384, 256], P('row'), may hold values from -6 to 6
Outputs:
- maps_out: float32 [4, 2048, 256], P('view', 'row')
- shared_out: float32 [16384, 256], P('row')
All inputs are finite; a program needn't handle non-finite values.
Results may differ from a plain program's by a relative error of at most 0.00013.
Values sent between devices are 32-bit elements; how exact they have to be, the bound alone decides.
A program may use at most 128 MiB of HBM per device.

v0:
```python
import jax
import jax.numpy as jnp
from jax import lax
from jax.sharding import PartitionSpec as P

ITERS = 2
NEWTON = 5


step_rate = 0.5


def newton_root(gram_matrix):
    highest = lax.Precision.HIGHEST
    frob_norm = jnp.sqrt(jnp.sum(gram_matrix * gram_matrix))
    scaled = gram_matrix / frob_norm
    identity = jnp.eye(gram_matrix.shape[0], dtype=jnp.float32)
    inverse_root = identity
    for newton_step in range(NEWTON):
        correction = 1.5 * identity - 0.5 * jnp.dot(inverse_root, scaled, precision=highest)
        scaled = jnp.dot(scaled, correction, precision=highest)
        inverse_root = jnp.dot(correction, inverse_root, precision=highest)
    return (inverse_root, frob_norm)


def local(features, view_maps, shared):
    highest = lax.Precision.HIGHEST
    samples = features[0]
    map_shard = view_maps[0]
    local_rows = samples.shape[0]
    width = samples.shape[1]
    shard_rows = map_shard.shape[0]
    total_rows = local_rows * lax.axis_size("row")
    view_count = lax.axis_size("view")
    step_size = step_rate * width / total_rows
    whole_map = lax.all_gather(map_shard, "row", axis=0, tiled=True)
    projected = jnp.dot(samples, whole_map, precision=highest)
    for iteration in range(ITERS):
        residual = projected - shared
        gradient = lax.psum(jnp.dot(samples.T, residual, precision=highest), "row")
        whole_map = whole_map - step_size * gradient
        projected = jnp.dot(samples, whole_map, precision=highest)
        average = lax.psum(projected, "view") / view_count
        gram_matrix = lax.psum(jnp.dot(average.T, average, precision=highest), "row")
        inverse_root, frob_norm = newton_root(gram_matrix)
        shared = jnp.dot(average, inverse_root, precision=highest) * jnp.sqrt(
            total_rows / frob_norm
        )
    map_shard = lax.dynamic_slice_in_dim(
        whole_map, lax.axis_index("row") * shard_rows, shard_rows, 0
    )
    return (map_shard[None], shared)


def solution(mesh):
    in_specs = (P("view", "row", None), P("view", "row", None), P("row", None))
    out_specs = (P("view", "row", None), P("row", None))
    return jax.shard_map(local, mesh=mesh, in_specs=in_specs, out_specs=out_specs, check_vma=False)
```

profile of v0, /device:TPU:0, one launch (start us, length us, event | category | flops | bytes accessed | tf_op | source)
XLA Modules:
  0.0 663.0 jit_solution(7803501747945105830)
XLA Ops:
  7.2 1.8 copy.6
  9.1 54.6 %all-gather.3.cloned.1.call-done = f32[1,2048,256]{1,2,0:T(8,128)} async-done(((f32[1,256,256]{1,2,0:T(8,128)}), f32[1,2048,256]{1,2,0:T(8,128)}) %all-gather.3.cloned.1.call-update) | async-done | bytes 2097168 | tf_op jit(solution)/shard_map/all_gather | solution.py:36
  63.7 17.4 %fusion.23 = f32[2048,256]{1,0:T(8,128)S(1)} fusion(f32[2048,256]{1,0:T(8,128)} %param.5, f32[1,2048,2048]{2,1,0:T(8,128)} %param.3, f32[1,2048,256]{1,2,0:T(8,128)} %all-gather.3.cloned.1.call-done), kind=kOutput, calls=%fused_computation.17 | convolution fusion | flops 12885426176 | bytes 23068672 | tf_op jit(solution)/shard_map/dot_general | solution.py:37
  81.1 31.3 %fusion.10 = f32[2048,256]{0,1:T(8,128)} fusion(f32[2048,256]{1,0:T(8,128)S(1)} %fusion.23, f32[1,2048,2048]{2,1,0:T(8,128)S(1)} %copy-done), kind=kOutput, calls=%fused_computation.10 | convolution fusion | flops 12884901888 | bytes 20971520 | tf_op jit(solution)/shard_map/dot_general | solution.py:40
  112.5 100.6 %all-reduce.7.cloned.1.call-done = f32[2048,256]{0,1:T(8,128)} async-done(((f32[2048,256]{0,1:T(8,128)}), f32[2048,256]{0,1:T(8,128)}) %all-reduce.7.cloned.1.call-update) | async-done | bytes 2097168 | tf_op jit(solution)/shard_map/psum | solution.py:40
  213.1 18.8 %fusion.13 = f32[2048,256]{0,1:T(8,128)} fusion(f32[1,2048,2048]{2,1,0:T(8,128)} %param.3, f32[1,2048,256]{1,2,0:T(8,128)S(1)} %copy-done.1, f32[2048,256]{0,1:T(8,128)} %all-reduce.7.cloned.1.call-done), kind=kOutput, calls=%fused_computation.11 | convolution fusion | flops 12885950464 | bytes 23068672 | tf_op jit(solution)/shard_map/dot_general | solution.py:42
  232.0 50.8 %all-reduce.9.cloned.1.call-done = f32[2048,256]{0,1:T(8,128)} async-done(((f32[2048,256]{0,1:T(8,128)}), f32[2048,256]{0,1:T(8,128)}) %all-reduce.9.cloned.1.call-update) | async-done | bytes 2097168 | tf_op jit(solution)/shard_map/psum | solution.py:43
  282.8 4.9 fusion.31
  287.7 71.2 %all-reduce.11.cloned.1.call-done = f32[256,256]{1,0:T(8,128)} async-done(((f32[256,256]{1,0:T(8,128)}), f32[256,256]{1,0:T(8,128)}) %all-reduce.11.cloned.1.call-update) | async-done | bytes 262160 | tf_op jit(solution)/shard_map/psum | solution.py:44
  358.9 1.6 multiply_reduce_fusion.1
  361.3 1.3 fusion.42
  362.8 1.3 fusion.49
  368.5 4.4 fusion.22
  372.9 17.8 %fusion.16 = f32[2048,256]{0,1:T(8,128)} fusion(f32[2048,256]{0,1:T(8,128)S(1)} %fusion.22, f32[1,2048,2048]{2,1,0:T(8,128)} %param.3), kind=kOutput, calls=%fused_computation.12 | convolution fusion | flops 12884901888 | bytes 20971520 | tf_op jit(solution)/shard_map/dot_general | solution.py:40
  390.7 101.6 %all-reduce.13.cloned.1.call-done = f32[2048,256]{0,1:T(8,128)} async-done(((f32[2048,256]{0,1:T(8,128)}), f32[2048,256]{0,1:T(8,128)}) %all-reduce.13.cloned.1.call-update) | async-done | bytes 2097168 | tf_op jit(solution)/shard_map/psum | solution.py:40
  492.4 2.8 multiply_subtract_fusion
  495.2 1.3 copy-done.2
  496.5 17.9 %fusion.19 = f32[2048,256]{0,1:T(8,128)} fusion(f32[2048,256]{0,1:T(8,128)S(1)} %multiply_subtract_fusion, f32[1,2048,2048]{2,1,0:T(8,128)} %param.3), kind=kOutput, calls=%fused_computation.13 | convolution fusion | flops 12884901888 | bytes 20971520 | tf_op jit(solution)/shard_map/dot_general | solution.py:42
  514.7 50.6 %all-reduce.15.cloned.1.call-done = f32[2048,256]{0,1:T(8,128)} async-done(((f32[2048,256]{0,1:T(8,128)}), f32[2048,256]{0,1:T(8,128)}) %all-reduce.15.cloned.1.call-update) | async-done | bytes 2097168 | tf_op jit(solution)/shard_map/psum | solution.py:43
  565.2 4.9 fusion.28
  572.0 69.4 %all-reduce.17.cloned.1.call-done = f32[256,256]{1,0:T(8,128)} async-done(((f32[256,256]{1,0:T(8,128)}), f32[256,256]{1,0:T(8,128)}) %all-reduce.17.cloned.1.call-update) | async-done | bytes 262160 | tf_op jit(solution)/shard_map/psum | solution.py:44
  641.4 1.6 multiply_reduce_fusion
  645.3 1.3 fusion.50
  651.0 4.8 convolution_multiply_fusion
  (48 shorter events, 12.6 us)
Async XLA Ops:
  7.2 56.5 %all-gather.3.cloned.1.call-start = ((), (), s32[]{:S(2)}) async-start(), calls=%async_computation.6 | async-start | bytes 2359296 | tf_op jit(solution)/shard_map/all_gather | solution.py:36
  9.0 204.1 %all-reduce.7.cloned.1.call-start = ((), (), s32[]{:S(2)}) async-start(), calls=%async_computation | async-start | bytes 4194304 | tf_op jit(solution)/shard_map/psum | solution.py:40
  63.7 17.4 %copy-start = (f32[1,2048,2048]{2,1,0:T(8,128)S(1)}, f32[1,2048,2048]{2,1,0:T(8,128)}, u32[]{:S(2)}) copy-start(f32[1,2048,2048]{2,1,0:T(8,128)} %param.3) | copy-start | bytes 50331652
  112.4 100.7 %copy-start.1 = (f32[1,2048,256]{1,2,0:T(8,128)S(1)}, f32[1,2048,256]{1,2,0:T(8,128)}, u32[]{:S(2)}) copy-start(f32[1,2048,256]{1,2,0:T(8,128)} %all-gather.3.cloned.1.call-done) | copy-start | bytes 6291460
  112.4 170.4 %all-reduce.9.cloned.1.call-start = ((), (), s32[]{:S(2)}) async-start(), calls=%async_computation.1 | async-start | bytes 4194304 | tf_op jit(solution)/shard_map/psum | solution.py:43
  231.9 127.0 %all-reduce.11.cloned.1.call-start = ((), (), s32[]{:S(2)}) async-start(), calls=%async_computation.2 | async-start | bytes 524288 | tf_op jit(solution)/shard_map/psum | solution.py:44
  287.7 204.7 %all-reduce.13.cloned.1.call-start = ((), (), s32[]{:S(2)}) async-start(), calls=%async_computation.3 | async-start | bytes 4194304 | tf_op jit(solution)/shard_map/psum | solution.py:40
  390.7 174.6 %all-reduce.15.cloned.1.call-start = ((), (), s32[]{:S(2)}) async-start(), calls=%async_computation.4 | async-start | bytes 4194304 | tf_op jit(solution)/shard_map/psum | solution.py:43
  495.2 1.3 copy-start.2
  514.4 127.0 %all-reduce.17.cloned.1.call-start = ((), (), s32[]{:S(2)}) async-start(), calls=%async_computation.5 | async-start | bytes 524288 | tf_op jit(solution)/shard_map/psum | solution.py:44
  648.9 2.0 copy-start.3
Sparse Core Ops, SparseCore 0:
  10.6 53.0 all-gather.2
  112.5 100.5 all-reduce.6
  232.1 50.6 all-reduce.8
  287.8 71.0 all-reduce.10
  390.8 101.5 all-reduce.12
  514.5 50.6 all-reduce.14
  570.3 71.0 all-reduce.16
where the time goes:
time: 667 us; the launch traced here: 663 us
  waiting for transfers between devices  499 us (75%)
  matrix products  136 us (20%)
  between operations  16.4 us (2%)
    psum x2, waiting for transfers between devices, local(): gradient = lax.psum(jnp.dot(samples.T, residual, precision=highest), 'row')  202 us
    psum x2, waiting for transfers between devices, local(): lax.psum(jnp.dot(average.T, average, precision=highest), 'row')  141 us
    psum x2, waiting for transfers between devices, local(): average = lax.psum(projected, 'view') / view_count  101 us
    all_gather x1, waiting for transfers between devices, local(): whole_map = lax.all_gather(map_shard, 'row', axis=0, tiled=True)  54.6 us
    dot_general x3, matrix products, local(): projected = jnp.dot(samples, whole_map, precision=highest)  54.1 us
    dot_general x2, matrix products, local(): gradient = lax.psum(jnp.dot(samples.T, residual, precision=highest), 'row')  49.1 us
  transfers between devices with their start and end apart: 7, of which 7 were waited for; matrix products, arithmetic and copies ran while one was open for 0% of the time, Pallas kernels for 0%

commit v1 on v0

v1 whole, which is shorter than its diff:
```python
import functools
import math

import jax
import jax.numpy as jnp
from jax import lax
from jax.experimental import pallas as pl
from jax.experimental.pallas import tpu as pltpu
from jax.sharding import PartitionSpec as P

ITERS = 2
NEWTON = 5
STEP_RATE = 0.5
CORES = 2
MESH = pl.DeviceIdType.MESH
F32 = jnp.float32
BF16 = jnp.bfloat16


def split(x):
    hi = x.astype(BF16)
    return hi, (x - hi.astype(F32)).astype(BF16)


def dot3s(a, b):
    lhs = jnp.concatenate([a[0], a[1], a[0]], axis=1)
    rhs = jnp.concatenate([b[0], b[0], b[1]], axis=0)
    return jnp.dot(lhs, rhs, preferred_element_type=F32)


def dot3(a, b):
    return dot3s(split(a), split(b))


def newton_root(gram):
    size = gram.shape[0]
    frob = jnp.sqrt(jnp.sum(gram * gram, keepdims=True))
    scaled = gram / frob
    rows = lax.broadcasted_iota(jnp.int32, (size, size), 0)
    cols = lax.broadcasted_iota(jnp.int32, (size, size), 1)
    eye = jnp.where(rows == cols, 1.0, 0.0).astype(F32)
    root = None
    for step in range(NEWTON):
        ym = split(scaled)
        zy = scaled if root is None else dot3s(split(root), ym)
        corr = 1.5 * eye - 0.5 * zy
        cs = split(corr)
        if step < NEWTON - 1:
            scaled = dot3s(ym, cs)
        root = corr if root is None else dot3s(cs, split(root))
    return root, frob


def kernel(
    dims,
    f_ref, w_ref, s_ref, wo_ref, so_ref,
    fhi, flo, fbuf, rthi, rtlo, y, wfull, gs, xr, zs, zr,
    vs, cr, yr, av, gram, gr, gv, gfull,
    f_sem, agz_s, agz_r, agx_s, agx_r, rsx_s, rsx_r, rsz_s, rsz_r,
    vrc_s, vrc_r, vry_s, vry_r, vgy_s, vgy_r, vgc_s, vgc_r,
    g1_s, g1_r, g2_s, g2_r, g3_s, g3_r,
):
    nz, nx, ny, nc = dims
    nrow, nview = nz * nx, ny * nc
    row, view = lax.axis_index("row"), lax.axis_index("view")
    z, x = row // nx, row % nx
    yy, core = view // nc, view % nc
    local = y.shape[0]
    width = f_ref.shape[2]
    keys = y.shape[1]
    shard = w_ref.shape[1]
    total = local * nrow
    step_size = STEP_RATE * width / total
    chunk = fbuf.shape[1]
    nchunk = local // chunk
    part = local // nview
    gpart = keys // nrow

    def at_row(zz, xx):
        return {"row": zz * nx + xx}

    def at_view(y1, c1):
        return {"view": y1 * nc + c1}

    def zmod(d):
        return lax.rem(z + d + nz, nz)

    def xmod(d):
        return lax.rem(x + d + nx, nx)

    def ymod(d):
        return lax.rem(yy + d + ny, ny)

    def cmod(d):
        return lax.rem(core + d + nc, nc)

    pending = []

    def send(src, dst, ssem, rsem, dev):
        copy = pltpu.make_async_remote_copy(
            src_ref=src, dst_ref=dst, send_sem=ssem, recv_sem=rsem,
            device_id=dev, device_id_type=MESH,
        )
        copy.start()
        pending.append(copy)

    def recv(buf, ssem, rsem, dev):
        pltpu.make_async_remote_copy(
            src_ref=buf, dst_ref=buf, send_sem=ssem, recv_sem=rsem,
            device_id=dev, device_id_type=MESH,
        ).wait_recv()

    def flush():
        for copy in pending:
            copy.wait_send()
        pending.clear()

    def load(c):
        return pltpu.make_async_copy(
            f_ref.at[0, pl.ds(c * chunk, chunk)], fbuf.at[c % 2], f_sem.at[c % 2]
        )

    load(0).start()
    wfull[0, row] = w_ref[0]
    barrier = pltpu.get_barrier_semaphore()
    for d in range(1, nrow):
        pl.semaphore_signal(
            barrier, inc=1, device_id={"row": lax.rem(row + d, nrow)}, device_id_type=MESH
        )
    for d in range(1, nview):
        pl.semaphore_signal(
            barrier, inc=1, device_id={"view": lax.rem(view + d, nview)}, device_id_type=MESH
        )
    pl.semaphore_wait(barrier, nrow + nview - 2)

    def gather_start(g):
        own = wfull.at[g, row]
        for dx in range(1, nx):
            send(own, own, agx_s.at[g, 0, dx], agx_r.at[g, 0, dx], at_row(z, xmod(dx)))
        for dz in range(1, nz):
            send(own, own, agz_s.at[g, dz], agz_r.at[g, dz], at_row(zmod(dz), x))

    def project(g, block, first):
        ws = split(wfull[g, block])
        rhs = jnp.concatenate([ws[0], ws[0], ws[1]], axis=0)

        @pl.loop(0, local // 512)
        def _(c):
            rows = pl.ds(pl.multiple_of(c * 512, 512), 512)
            hi, lo = fhi[block, rows], flo[block, rows]
            out = jnp.dot(
                jnp.concatenate([hi, lo, hi], axis=1), rhs, preferred_element_type=F32
            )
            if first:
                y[rows] = out
            else:
                y[rows] += out

    def gather_project(g):
        project(g, row, True)
        for dz in range(nz):
            zsrc = zmod(-dz)
            if dz:
                block = zsrc * nx + x
                got = wfull.at[g, block]
                recv(got, agz_s.at[g, dz], agz_r.at[g, dz], at_row(zsrc, x))
                for dx in range(1, nx):
                    send(
                        got, got, agx_s.at[g, dz, dx], agx_r.at[g, dz, dx],
                        at_row(z, xmod(dx)),
                    )
                project(g, block, False)
            prev = dz - 1
            if prev >= 0:
                x_part(g, prev)
        x_part(g, nz - 1)

    def x_part(g, dz):
        for dx in range(1, nx):
            xsrc = xmod(-dx)
            block = zmod(-dz) * nx + xsrc
            recv(
                wfull.at[g, block], agx_s.at[g, dz, dx], agx_r.at[g, dz, dx],
                at_row(z, xsrc),
            )
            project(g, block, False)

    def set_residual(shared_of):
        @pl.loop(0, local // 512)
        def _(c):
            rows = pl.ds(pl.multiple_of(c * 512, 512), 512)
            res = (y[rows] - shared_of(c, rows)).T
            hi, lo = split(res)
            rthi[:, rows] = hi
            rtlo[:, rows] = lo

    def gradient(block):
        hi, lo = fhi[block], flo[block]
        rh = rthi[...]
        out = jnp.dot(rh, hi, preferred_element_type=F32)
        out += jnp.dot(rh, lo, preferred_element_type=F32)
        out += jnp.dot(rtlo[...], hi, preferred_element_type=F32)
        return out

    def scatter_gradient(it):
        order = list(range(1, nz)) + [0]
        for dz in order:
            for dx in range(1, nx):
                xt = xmod(dx)
                gs[it, dz, dx] = gradient(zmod(dz) * nx + xt)
                send(
                    gs.at[it, dz, dx], xr.at[it, dz, dx],
                    rsx_s.at[it, dz, dx], rsx_r.at[it, dz, dx], at_row(z, xt),
                )
        acc = None
        for dz in order:
            zs[it, dz] = gradient(zmod(dz) * nx + x)
            for dx in range(1, nx):
                recv(
                    xr.at[it, dz, dx], rsx_s.at[it, dz, dx], rsx_r.at[it, dz, dx],
                    at_row(z, xmod(-dx)),
                )
                zs[it, dz] += xr[it, dz, dx]
            if dz:
                send(
                    zs.at[it, dz], zr.at[it, dz], rsz_s.at[it, dz], rsz_r.at[it, dz],
                    at_row(zmod(dz), x),
                )
        acc = zs[it, 0]
        for dz in range(1, nz):
            recv(
                zr.at[it, dz], rsz_s.at[it, dz], rsz_r.at[it, dz], at_row(zmod(-dz), x)
            )
            acc = acc + zr[it, dz]
        wfull[it + 1, row] = wfull[it, row] - step_size * acc.T

    def yblock(block):
        return pl.ds(pl.multiple_of(block * part, part), part)

    def view_average(it):
        order = list(range(1, ny)) + [0]
        for dy in order:
            for dc in range(1, nc):
                ct = cmod(dc)
                send(
                    y.at[yblock(ymod(dy) * nc + ct)], cr.at[it, dy, dc],
                    vrc_s.at[it, dy, dc], vrc_r.at[it, dy, dc], at_view(yy, ct),
                )
        for dy in order:
            acc = y[yblock(ymod(dy) * nc + core)]
            for dc in range(1, nc):
                recv(
                    cr.at[it, dy, dc], vrc_s.at[it, dy, dc], vrc_r.at[it, dy, dc],
                    at_view(yy, cmod(-dc)),
                )
                acc = acc + cr[it, dy, dc]
            vs[it, dy] = acc
            if dy:
                send(
                    vs.at[it, dy], yr.at[it, dy], vry_s.at[it, dy], vry_r.at[it, dy],
                    at_view(ymod(dy), core),
                )
        acc = vs[it, 0]
        for dy in range(1, ny):
            recv(
                yr.at[it, dy], vry_s.at[it, dy], vry_r.at[it, dy],
                at_view(ymod(-dy), core),
            )
            acc = acc + yr[it, dy]
        acc = acc / nview
        av[it, view] = acc
        own = av.at[it, view]
        for dy in range(1, ny):
            send(
                own, own, vgy_s.at[it, dy], vgy_r.at[it, dy], at_view(ymod(dy), core)
            )
        for dc in range(1, nc):
            send(
                own, own, vgc_s.at[it, 0, dc], vgc_r.at[it, 0, dc], at_view(yy, cmod(dc))
            )

    def reduce_gram(it):
        own = av[it, view]
        hi, lo = split(own)
        thi, tlo = split(own.T)
        gram[it] = dot3s((thi, tlo), (hi, lo)).reshape(nrow, gpart, keys)
        for d in range(1, nrow):
            to = lax.rem(row + d, nrow)
            send(
                gram.at[it, to], gr.at[it, d], g1_s.at[it, d], g1_r.at[it, d], {"row": to}
            )
        acc = gram[it, row]
        for d in range(1, nrow):
            recv(
                gr.at[it, d], g1_s.at[it, d], g1_r.at[it, d],
                {"row": lax.rem(row - d + nrow, nrow)},
            )
            acc = acc + gr[it, d]
        gv[it, 0] = acc
        for d in range(1, nview):
            send(
                gv.at[it, 0], gv.at[it, d], g2_s.at[it, d], g2_r.at[it, d],
                {"view": lax.rem(view + d, nview)},
            )
        acc = gv[it, 0]
        for d in range(1, nview):
            recv(
                gv.at[it, d], g2_s.at[it, d], g2_r.at[it, d],
                {"view": lax.rem(view - d + nview, nview)},
            )
            acc = acc + gv[it, d]
        gfull[it, row] = acc
        mine = gfull.at[it, row]
        for d in range(1, nrow):
            send(
                mine, mine, g3_s.at[it, d], g3_r.at[it, d],
                {"row": lax.rem(row + d, nrow)},
            )

    def forward_average(it):
        for dy in range(1, ny):
            ysrc = ymod(-dy)
            got = av.at[it, ysrc * nc + core]
            recv(got, vgy_s.at[it, dy], vgy_r.at[it, dy], at_view(ysrc, core))
            for dc in range(1, nc):
                send(
                    got, got, vgc_s.at[it, dy, dc], vgc_r.at[it, dy, dc],
                    at_view(yy, cmod(dc)),
                )

    def finish_average(it):
        for dy in range(ny):
            for dc in range(1, nc):
                csrc = cmod(-dc)
                recv(
                    av.at[it, ymod(-dy) * nc + csrc],
                    vgc_s.at[it, dy, dc], vgc_r.at[it, dy, dc], at_view(yy, csrc),
                )

    def finish_gram(it):
        for d in range(1, nrow):
            src = lax.rem(row - d + nrow, nrow)
            recv(gfull.at[it, src], g3_s.at[it, d], g3_r.at[it, d], {"row": src})
        return newton_root(gfull[it].reshape(keys, keys))

    gather_start(0)
    for c in range(nchunk):
        if c + 1 < nchunk:
            load(c + 1).start()
        load(c).wait()
        for b in range(nrow):
            hi, lo = split(fbuf[c % 2, :, b * shard:(b + 1) * shard])
            fhi[b, c * chunk:(c + 1) * chunk] = hi
            flo[b, c * chunk:(c + 1) * chunk] = lo
    gather_project(0)
    set_residual(lambda c, rows: s_ref[rows])
    for it in range(ITERS):
        scatter_gradient(it)
        gather_start(it + 1)
        gather_project(it + 1)
        view_average(it)
        reduce_gram(it)
        forward_average(it)
        root, frob = finish_gram(it)
        scale = jnp.sqrt(total / frob)
        finish_average(it)
        flush()
        rs = split(root)
        if it < ITERS - 1:
            for v in range(nview):
                rows = slice(v * part, (v + 1) * part)
                hi, lo = split((y[rows] - dot3s(split(av[it, v]), rs) * scale).T)
                rthi[:, rows] = hi
                rtlo[:, rows] = lo
        else:
            for v in range(nview):
                so_ref[v * part:(v + 1) * part] = dot3s(split(av[it, v]), rs) * scale
            wo_ref[0] = wfull[ITERS, row]


def solution(mesh):
    nrow, nview = mesh.shape["row"], mesh.shape["view"]
    nx = max(d for d in range(1, math.isqrt(nrow) + 1) if nrow % d == 0)
    nz = nrow // nx
    nc = CORES if nview % CORES == 0 else 1
    ny = nview // nc

    def local(features, view_maps, shared):
        rows, width = features.shape[1], features.shape[2]
        shard, keys = view_maps.shape[1], view_maps.shape[2]
        part, gpart = rows // nview, keys // nrow
        chunk = 256
        dma = pltpu.SemaphoreType.DMA
        sems = []
        for shape in [
            (ITERS + 1, nz), (ITERS + 1, nz, nx), (ITERS, nz, nx), (ITERS, nz),
            (ITERS, ny, nc), (ITERS, ny), (ITERS, ny), (ITERS, ny, nc),
            (ITERS, nrow), (ITERS, nview), (ITERS, nrow),
        ]:
            sems += [dma(shape), dma(shape)]
        vmem = pl.BlockSpec(memory_space=pltpu.VMEM)
        return pl.pallas_call(
            functools.partial(kernel, (nz, nx, ny, nc)),
            out_shape=(
                jax.ShapeDtypeStruct(view_maps.shape, F32),
                jax.ShapeDtypeStruct(shared.shape, F32),
            ),
            in_specs=[pl.BlockSpec(memory_space=pl.ANY), vmem, vmem],
            out_specs=(vmem, vmem),
            scratch_shapes=[
                pltpu.VMEM((nrow, rows, shard), BF16),
                pltpu.VMEM((nrow, rows, shard), BF16),
                pltpu.VMEM((2, chunk, width), F32),
                pltpu.VMEM((keys, rows), BF16),
                pltpu.VMEM((keys, rows), BF16),
                pltpu.VMEM((rows, keys), F32),
                pltpu.VMEM((ITERS + 1, nrow, shard, keys), F32),
                pltpu.VMEM((ITERS, nz, nx, keys, shard), F32),
                pltpu.VMEM((ITERS, nz, nx, keys, shard), F32),
                pltpu.VMEM((ITERS, nz, keys, shard), F32),
                pltpu.VMEM((ITERS, nz, keys, shard), F32),
                pltpu.VMEM((ITERS, ny, part, keys), F32),
                pltpu.VMEM((ITERS, ny, nc, part, keys), F32),
                pltpu.VMEM((ITERS, ny, part, keys), F32),
                pltpu.VMEM((ITERS, nview, part, keys), F32),
                pltpu.VMEM((ITERS, nrow, gpart, keys), F32),
                pltpu.VMEM((ITERS, nrow, gpart, keys), F32),
                pltpu.VMEM((ITERS, nview, gpart, keys), F32),
                pltpu.VMEM((ITERS, nrow, gpart, keys), F32),
                dma((2,)),
            ] + sems,
            compiler_params=pltpu.CompilerParams(
                collective_id=0, has_side_effects=True, vmem_limit_bytes=67043328
            ),
        )(features, view_maps, shared)

    in_specs = (P("view", "row", None), P("view", "row", None), P("row", None))
    out_specs = (P("view", "row", None), P("row", None))
    return jax.shard_map(local, mesh=mesh, in_specs=in_specs, out_specs=out_specs, check_vma=False)
```

time: 667 us -> 265 us (0.40)
  waiting for transfers between devices: 499 us -> 0 us
  Pallas kernels: 0 us -> 259 us
  matrix products: 136 us -> 0 us
  between operations: 16.4 us -> 0.64 us
    psum x6 -> x0, waiting for transfers between devices: 444 us -> none  [the longest x2 202 us: local(): gradient = lax.psum(jnp.dot(samples.T, residual, precision=highest), 'row')]
    pallas_call x0 -> x1, Pallas kernels: none -> 259 us  [local(): pl.pallas_call(functools.partial(kernel, (nz, nx, ny, nc)), out_shape=(ja...]
    dot_general x37 -> x0, matrix products: 136 us -> none  [the longest x3 54.1 us: local(): projected = jnp.dot(samples, whole_map, precision=highest)]
    all_gather x1 -> x0, waiting for transfers between devices: 54.6 us -> none  [local(): whole_map = lax.all_gather(map_shard, 'row', axis=0, tiled=True)]
  transfers between devices with their start and end apart: 7 -> 0, of which waited for: 7 -> 0; matrix products, arithmetic and copies ran while one was open for 0% -> 0% of each run, Pallas kernels for 0% -> 0%
where the time goes in v1:
time: 265 us
  Pallas kernels  259 us (98%)
  local copies, waits for them, and re-layouts  4.71 us (2%)
    pallas_call x1, Pallas kernels, local(): pl.pallas_call(functools.partial(kernel, (nz, nx, ny, nc)), out_shape=(ja...  259 us

profile of v1, /device:TPU:0, one launch (start us, length us, event | category | flops | bytes accessed | tf_op | source)
XLA Modules:
  0.0 264.6 jit_solution(4421589634857526854)
XLA Ops:
  0.6 259.3 %shard_map.50 = (f32[1,256,256]{2,1,0:T(8,128)}, f32[2048,256]{1,0:T(8,128)}) custom-call(f32[1,2048,2048]{2,1,0:T(8,128)} %f_ref.1, f32[1,256,256]{2,1,0:T(8,128)} %w_ref.1, f32[2048,256]{1,0:T(8,128)} %s_ref.1), custom_call_target="tpu_custom_call" | custom-call | tf_op jit(solution)/shard_map/pallas_call | solution.py:402
  259.9 1.7 copy.7
  261.6 3.0 %copy.8 = f32[2048,256]{1,0:T(8,128)} copy(f32[2048,256]{1,0:T(8,128)} %get-tuple-element.5) | data formatting | bytes 4194304
